TPU v7x, 512 devices: a whole 4x4x16 slice. The times are simulated.
512 devices in a mesh: dp: 16 (over x, y), heads: 16 (over z), side: 2 (over core).
Axes of the slice: x: 4, y: 4, z: 16, core: 2. Of those that a mesh axis runs over, the one named last changes fastest.
Arguments:
- queries: bfloat16 [384, 2, 4096], P('dp', None, ('heads', 'side')), may hold values from -6 to 6
- new_keys: bfloat16 [384, 2, 4096], P('dp', None, ('heads', 'side')), may hold values from -6 to 6
- new_values: bfloat16 [384, 2, 4096], P('dp', None, ('heads', 'side')), may hold values from -6 to 6
- head_states: bfloat16 [384, 32, 128, 128], P('dp', ('heads', 'side')), may hold values from -6 to 6
- slopes: float32 [32], P(('heads', 'side')), may hold values from 0.004 to 0.9
- head_gain: float32 [4096], P(('heads', 'side')), may hold values from 0.5 to 1.5
- out_weight: bfloat16 [4096, 3072], P(('heads', 'side')), may hold values from -0.1875 to 0.1875
- residual: bfloat16 [384, 2, 3072], P('dp', None, ('heads', 'side')), may hold values from -10 to 10
- norm_gain: float32 [3072], replicated, may hold values from 0.5 to 1.5
- expert_ids: int32 [384, 2, 2], P('dp'), may hold values from 0 to 15, all different within a row; in each aligned block of 48 rows (0 to 47, 48 to 95, ..., all dimensions but the last counted through in order) at most 9 rows name the same one
- expert_gates: float32 [384, 2, 2], P('dp'), may hold values from 0.2 to 1
- w_gate: bfloat16 [16, 16, 192, 4608], P('dp', None, 'side', 'heads'), may hold values from -0.109375 to 0.109375
- w_up: bfloat16 [16, 16, 192, 4608], P('dp', None, 'side', 'heads'), may hold values from -0.109375 to 0.109375
- w_down: bfloat16 [16, 4608, 16, 192], P('dp', 'heads', None, 'side'), may hold values from -0.125 to 0.125
Outputs:
- state_out: bfloat16 [384, 32, 128, 128], P('dp', ('heads', 'side'))
- resid_out: bfloat16 [384, 2, 3072], P('dp', None, ('heads', 'side'))
- moe_out: bfloat16 [384, 2, 3072], P('dp', None, ('heads', 'side'))
Inputs may be any that keep to these rules, and one draw needn't show every extreme that they name: `expert_ids`: among the 48 tokens of one dp index a token's 2 experts differ, no expert is chosen by more than 9 of them, and some expert is chosen by exactly 9.
All inputs are finite; a program needn't handle non-finite values.
Results may differ from a plain program's by a relative error of at most 0.025.
Values may be sent and summed in bfloat16 or wider, within the bound.
A program may use at most 64 MiB of HBM per device.

v0:
```python
import jax
import jax.numpy as jnp
from jax import lax
from jax.sharding import PartitionSpec as P


def local(
    queries,
    new_keys,
    new_values,
    head_states,
    slopes,
    head_gain,
    out_weight,
    residual,
    norm_gain,
    expert_ids,
    expert_gates,
    w_gate,
    w_up,
    w_down,
):
    requests_dev, step_count, inner_width = queries.shape
    local_heads = slopes.shape[0]
    head_size = inner_width // local_heads
    query_rows = queries.astype(jnp.float32).reshape(
        requests_dev, step_count, local_heads, head_size
    )
    key_rows = new_keys.astype(jnp.float32).reshape(
        requests_dev, step_count, local_heads, head_size
    )
    value_rows = new_values.astype(jnp.float32).reshape(
        requests_dev, step_count, local_heads, head_size
    )
    decays = jnp.exp(-slopes)[None, :, None, None]
    current = head_states.astype(jnp.float32)
    outputs = []
    for step in range(step_count):
        current = decays * current + key_rows[:, step, :, :, None] * value_rows[:, step, :, None, :]
        outputs.append(
            jnp.einsum(
                "rhi,rhij->rhj", query_rows[:, step], current, precision=lax.Precision.HIGHEST
            )
        )
    state_out = current.astype(jnp.bfloat16)
    head_output = jnp.stack(outputs, 1)
    scaled = head_output * lax.rsqrt(jnp.mean(head_output * head_output, -1, keepdims=True) + 1e-06)
    tokens_dev = requests_dev * step_count
    normed = (
        (scaled * head_gain.reshape(local_heads, head_size))
        .astype(jnp.bfloat16)
        .reshape(tokens_dev, inner_width)
    )
    partial_out = jnp.dot(normed, out_weight, preferred_element_type=jnp.float32)
    attention = lax.psum_scatter(partial_out, ("heads", "side"), scatter_dimension=1, tiled=True)
    width = norm_gain.shape[0]
    piece_width = attention.shape[1]
    resid_new = (residual.reshape(tokens_dev, piece_width).astype(jnp.float32) + attention).astype(
        jnp.bfloat16
    )
    stream = resid_new.astype(jnp.float32)
    sum_squares = lax.psum(jnp.sum(stream * stream, 1), ("heads", "side"))
    gain_piece = lax.dynamic_slice_in_dim(
        norm_gain, lax.axis_index(("heads", "side")) * piece_width, piece_width
    )
    mixed_in = (stream * lax.rsqrt(sum_squares / width + 1e-06)[:, None] * gain_piece).astype(
        jnp.bfloat16
    )
    groups = lax.axis_size("dp")
    heads_count = lax.axis_size("heads")
    choices_each = expert_ids.shape[2]
    capacity = max(2, 3 * choices_each * tokens_dev // (2 * groups))
    flat_ids = expert_ids.reshape(-1)
    onehot_table = (flat_ids[:, None] == jnp.arange(groups, dtype=jnp.int32)[None, :]).astype(
        jnp.int32
    )
    earlier = jnp.cumsum(onehot_table, 0) - onehot_table
    slot_index = jnp.sum(earlier * onehot_table, 1)
    target = flat_ids * capacity + slot_index
    source_row = jnp.arange(tokens_dev * choices_each, dtype=jnp.int32) // choices_each
    gate_flat = w_gate[0].reshape(-1, w_gate.shape[3])
    up_flat = w_up[0].reshape(-1, w_up.shape[3])
    down_flat = w_down[0].reshape(w_down.shape[1], -1)
    holder = jnp.zeros((groups * capacity, mixed_in.shape[1]), mixed_in.dtype)
    arrived = lax.all_to_all(
        holder.at[target].set(mixed_in[source_row]).reshape(groups, capacity, mixed_in.shape[1]),
        "dp",
        split_axis=0,
        concat_axis=0,
        tiled=True,
    )
    piece = lax.all_gather(arrived, "heads", axis=2, tiled=True)
    flat_piece = piece.reshape(-1, piece.shape[2])
    gate_part = jnp.dot(flat_piece, gate_flat, preferred_element_type=jnp.float32)
    up_part = jnp.dot(flat_piece, up_flat, preferred_element_type=jnp.float32)
    gate_val, up_val = (
        lax.psum(gate_part.astype(jnp.bfloat16), "side").astype(jnp.float32),
        lax.psum(up_part.astype(jnp.bfloat16), "side").astype(jnp.float32),
    )
    activation = (jax.nn.silu(gate_val) * up_val).astype(jnp.bfloat16)
    down_part = jnp.dot(activation, down_flat, preferred_element_type=jnp.float32).reshape(
        groups, capacity, heads_count, piece_width
    )
    reduced = lax.psum_scatter(
        down_part.astype(jnp.bfloat16), "heads", scatter_dimension=2, tiled=True
    )
    returned = lax.all_to_all(reduced, "dp", split_axis=0, concat_axis=0, tiled=True)
    picked = returned.reshape(groups * capacity, piece_width)[target].astype(jnp.float32)
    weighted = picked * expert_gates.reshape(-1)[:, None]
    moe_out = jnp.sum(weighted.reshape(tokens_dev, choices_each, piece_width), 1).astype(
        jnp.bfloat16
    )
    return (
        state_out,
        resid_new.reshape(requests_dev, step_count, piece_width),
        moe_out.reshape(requests_dev, step_count, piece_width),
    )


def solution(mesh):
    return jax.shard_map(
        local,
        mesh=mesh,
        in_specs=(
            P("dp", None, ("heads", "side")),
            P("dp", None, ("heads", "side")),
            P("dp", None, ("heads", "side")),
            P("dp", ("heads", "side"), None, None),
            P(("heads", "side")),
            P(("heads", "side")),
            P(("heads", "side"), None),
            P("dp", None, ("heads", "side")),
            P(),
            P("dp", None, None),
            P("dp", None, None),
            P("dp", None, "side", "heads"),
            P("dp", None, "side", "heads"),
            P("dp", "heads", None, "side"),
        ),
        out_specs=(
            P("dp", ("heads", "side"), None, None),
            P("dp", None, ("heads", "side")),
            P("dp", None, ("heads", "side")),
        ),
        check_vma=False,
    )
```

profile of v0, /device:TPU:32, one launch (start us, length us, event | category | flops | bytes accessed | tf_op | source)
XLA Modules:
  0.0 491.2 jit_solution(13953203980056573112)
XLA Ops:
  7.2 0.8 bitcast_convert_fusion.1
  8.1 0.7 bitcast_convert_fusion
  9.6 0.7 copy.73
  10.3 2.2 fusion.5
  12.5 1.8 fusion.8
  14.3 0.1 multiply_reduce_fusion
  14.4 0.1 rsqrt.15
  14.6 1.6 convolution_bitcast_fusion
  16.3 0.1 copy.43
  16.4 0.1 eq.15
  16.5 0.1 fusion.26
  16.6 0.1 reduce_window_sum.11
  16.7 0.1 copy.42
  16.8 0.1 mul.182
  17.0 0.8 dynamic_slice.3
  17.8 0.2 select_reduce_fusion
  17.9 110.4 %reduce-scatter.7.cloned.1.call-done = f32[96,48]{1,0:T(8,128)} async-done(((f32[3072,48]{1,0:T(8,128)}), f32[96,48]{1,0:T(8,128)}) %reduce-scatter.7.cloned.1.call-update) | async-done | bytes 18448
  128.3 0.9 copy.61
  129.2 0.1 fusion.27
  129.3 46.0 %psum.21 = f32[48]{0:T(128)S(1)} all-reduce(f32[48]{0:T(128)S(1)} %get-tuple-element.5), channel_id=1, replica_groups=mesh['dp'=16,'heads'=16,'side'=2] {'heads','side'}, use_global_device_ids=true, to_apply=%region_5.6 | all-reduce | flops 48 | bytes 384 | tf_op jit(solution)/shard_map/psum | solution.py:62
  175.3 0.1 fusion.29
  175.4 1.0 scatter_custom_fusion
  176.5 0.1 reshape.300
  176.6 14.1 %all_to_all.10 = bf16[16,2,432]{2,1,0:T(2,128)(2,1)S(1)} all-to-all(bf16[16,2,432]{2,1,0:T(2,128)(2,1)S(1)} %reshape.300), channel_id=1, replica_groups=mesh['dp'=16,'heads'=16,'side'=2] {'dp'}, dimensions={0} | all-to-all | bytes 55296 | tf_op jit(solution)/shard_map/all_to_all | solution.py:85
  190.7 0.1 reshape.301
  190.8 0.4 copy.44
  191.2 83.1 %all_gather.3 = bf16[16,9,1536]{1,0,2:T(8,128)(2,1)} all-gather(bf16[16,9,96]{1,0,2:T(8,128)(2,1)S(1)} %copy.44), channel_id=1, replica_groups=mesh['dp'=16,'heads'=16,'side'=2] {'heads'}, dimensions={2}, use_global_device_ids=true | all-gather | bytes 470016 | tf_op jit(solution)/shard_map/all_gather | solution.py:92
  274.3 8.2 %reshape.288 = bf16[144,1536]{0,1:T(8,128)(2,1)S(1)} reshape(bf16[16,9,1536]{1,0,2:T(8,128)(2,1)} %all_gather.3) | data formatting | bytes 884736 | tf_op jit(solution)/shard_map/reshape | solution.py:93
  282.5 1.1 convolution_convert_fusion.1
  283.6 0.2 copy-done.1
  283.8 1.1 convolution_convert_fusion.2
  285.0 2.4 reshape_squeeze.11
  287.3 0.7 copy.46
  288.1 36.6 %all-reduce.7.cloned.1.call-done = (bf16[144,288]{1,0:T(8,128)(2,1)}, bf16[144,288]{1,0:T(8,128)(2,1)}) async-done(((bf16[144,288]{1,0:T(8,128)(2,1)}, bf16[144,288]{1,0:T(8,128)(2,1)}), (bf16[144,288]{1,0:T(8,128)(2,1)}, bf16[144,288]{1,0:T(8,128)(2,1)})) %all-reduce.7.cloned.1.call-update) | async-done | bytes 165904 | tf_op jit(solution)/shard_map/psum | solution.py:98
  324.7 1.0 fusion.23
  325.7 0.1 dot_general.29
  325.8 1.6 convolution_convert_fusion
  327.4 1.3 dynamic-slice
  328.7 1.7 fusion.4
  330.5 136.0 %all-reduce.5.cloned.1.call-done = bf16[16,9,16,96]{3,0,2,1:T(8,128)(2,1)} async-done(((bf16[16,9,16,96]{3,0,2,1:T(8,128)(2,1)}), bf16[16,9,16,96]{3,0,2,1:T(8,128)(2,1)}) %all-reduce.5.cloned.1.call-update) | async-done | bytes 442384
  466.5 1.4 constant_dynamic-slice_fusion
  467.9 0.7 reshape.302
  468.6 6.8 %all-to-all-start.1 = ((bf16[16,2,432]{2,1,0:T(2,128)(2,1)}), bf16[16,2,432]{2,1,0:T(2,128)(2,1)S(1)}, u32[]{:S(2)}, u32[]{:S(2)}) async-start(bf16[16,2,432]{2,1,0:T(2,128)(2,1)} %reshape.302), calls=%async_computation.1 | async-start | bytes 65536 | tf_op jit(solution)/shard_map/all_to_all | solution.py:107
  475.5 0.1 copy.59
  475.6 7.5 %all-to-all-done.1 = bf16[16,2,432]{2,1,0:T(2,128)(2,1)S(1)} async-done(((bf16[16,2,432]{2,1,0:T(2,128)(2,1)}), bf16[16,2,432]{2,1,0:T(2,128)(2,1)S(1)}, u32[]{:S(2)}, u32[]{:S(2)}) %all-to-all-start.1) | async-done | bytes 27680 | tf_op jit(solution)/shard_map/all_to_all | solution.py:107
  483.1 0.1 reshape.303
  483.2 0.7 gather_fusion
  483.9 0.7 fusion.25
  (38 shorter events, 0.4 us)
Async XLA Ops:
  7.2 275.4 %copy-start = (bf16[1,16,96,288]{3,2,1,0:T(8,128)(2,1)S(1)}, bf16[1,16,96,288]{3,2,1,0:T(8,128)(2,1)}, u32[]{:S(2)}) copy-start(bf16[1,16,96,288]{3,2,1,0:T(8,128)(2,1)} %param.26) | copy-start | bytes 2654212
  7.2 5.3 %copy-start.2 = (bf16[24,1,128,128]{3,2,1,0:T(8,128)(2,1)S(1)}, bf16[24,1,128,128]{3,2,1,0:T(8,128)(2,1)}, u32[]{:S(2)}) copy-start(bf16[24,1,128,128]{3,2,1,0:T(8,128)(2,1)} %param.17) | copy-start | bytes 2359300
  7.2 121.1 %reduce-scatter.7.cloned.1.call-start = ((), (), s32[]{:S(2)}) async-start(), calls=%async_computation.3 | async-start | bytes 1622016
  12.5 2.0 copy-start.4
  12.5 2.1 copy-start.9
  14.5 1.7 copy-start.7
  16.2 113.0 %copy-start.6 = (bf16[24,2,96]{2,1,0:T(2,128)(2,1)S(1)}, bf16[24,2,96]{2,1,0:T(2,128)(2,1)}, u32[]{:S(2)}) copy-start(bf16[24,2,96]{2,1,0:T(2,128)(2,1)} %param.21) | copy-start | bytes 27652
  16.2 308.5 %all-reduce.7.cloned.1.call-start = ((), (), s32[]{:S(2)}) async-start(), calls=%async_computation.5 | async-start | bytes 442368 | tf_op jit(solution)/shard_map/psum | solution.py:98
  129.3 145.0 %copy-start.5 = (bf16[48,96]{1,0:T(8,128)(2,1)}, bf16[48,96]{1,0:T(8,128)(2,1)S(1)}, u32[]{:S(2)}) copy-start(bf16[48,96]{1,0:T(8,128)(2,1)S(1)} %get-tuple-element.6) | copy-start | bytes 27652
  282.5 1.3 copy-start.1
  284.9 181.6 %all-reduce.5.cloned.1.call-start = ((), (), s32[]{:S(2)}) async-start(), calls=%async_computation.4 | async-start | bytes 1179648
  288.0 40.7 %copy-start.3 = (bf16[24,1,128,128]{3,2,1,0:T(8,128)(2,1)S(1)}, bf16[24,1,128,128]{3,2,1,0:T(8,128)(2,1)}, u32[]{:S(2)}) copy-start(bf16[24,1,128,128]{3,2,1,0:T(8,128)(2,1)} %param.17) | copy-start | bytes 2359300
  327.4 148.1 %copy-start.8 = (f32[24,2,2]{0,2,1:T(2,128)S(1)}, f32[24,2,2]{0,2,1:T(2,128)}, u32[]{:S(2)}) copy-start(f32[24,2,2]{0,2,1:T(2,128)} %param.24) | copy-start | bytes 1156
  468.6 14.4 %all-to-all-start.1 = ((bf16[16,2,432]{2,1,0:T(2,128)(2,1)}), bf16[16,2,432]{2,1,0:T(2,128)(2,1)S(1)}, u32[]{:S(2)}, u32[]{:S(2)}) async-start(bf16[16,2,432]{2,1,0:T(2,128)(2,1)} %reshape.302), calls=%async_computation.1 | async-start | bytes 65536 | tf_op jit(solution)/shard_map/all_to_all | solution.py:107
Sparse Core Ops, SparseCore 0:
  16.3 111.9 reduce-scatter.6
  285.0 39.6 all-reduce.6
  327.5 138.9 all-reduce.4
where the time goes:
time: 492 us; the launch traced here: 491 us
  waiting for transfers between devices  291 us (59%)
  blocking collectives  143 us (29%)
  local copies, waits for them, and re-layouts  20.6 us (4%)
  between operations  14.7 us (3%)
  matrix products  9.36 us (2%)
  starting transfers between devices  6.93 us (1%)
  other arithmetic  5.83 us (1%)
    unnamed x5, waiting for transfers between devices  246 us
    all_gather x1, blocking collectives, local(): piece = lax.all_gather(arrived, 'heads', axis=2, tiled=True)  83.1 us
    psum x1, blocking collectives, local(): sum_squares = lax.psum(jnp.sum(stream * stream, 1), ('heads', 'side'))  46 us
    psum x1, waiting for transfers between devices, local(): lax.psum(up_part.astype(jnp.bfloat16), 'side').astype(jnp.float32)  36.6 us
    all_to_all x1, blocking collectives, local(): lax.all_to_all(holder.at[target].set(mixed_in[source_row]).reshape(groups...  14.1 us
  transfers between devices with their start and end apart: 4, of which 4 were waited for; matrix products, arithmetic and copies ran while one was open for 2% of the time, Pallas kernels for 0%

commit v1 on v0

--- a/solution.py
+++ b/solution.py
@@ -89,7 +89,9 @@
         concat_axis=0,
         tiled=True,
     )
-    piece = lax.all_gather(arrived, "heads", axis=2, tiled=True)
+    piece = jnp.concatenate(
+        lax.all_to_all(jnp.stack([arrived] * lax.axis_size("heads")), "heads", 0, 0), axis=2
+    )
     flat_piece = piece.reshape(-1, piece.shape[2])
     gate_part = jnp.dot(flat_piece, gate_flat, preferred_element_type=jnp.float32)
     up_part = jnp.dot(flat_piece, up_flat, preferred_element_type=jnp.float32)

time: 492 us -> 434 us (0.88)
  blocking collectives: 143 us -> 105 us
  waiting for transfers between devices: 291 us -> 279 us
  local copies, waits for them, and re-layouts: 20.6 us -> 12.7 us
    all_gather x1 -> x0, blocking collectives: 83.1 us -> none  [local(): piece = lax.all_gather(arrived, 'heads', axis=2, tiled=True)]
    all_to_all x0 -> x1, blocking collectives: none -> 44.8 us  [local(): lax.all_to_all(jnp.stack([arrived] * lax.axis_size('heads')), 'heads', 0, 0)]
    psum x1, waiting for transfers between devices: 36.6 us -> 25.4 us  [local(): lax.psum(up_part.astype(jnp.bfloat16), 'side').astype(jnp.float32)]
    reshape x1, local copies, waits for them, and re-layouts: 8.24 us -> 0.15 us  [local(): jnp.concatenate(lax.all_to_all(jnp.stack([arrived] * lax.axis_size('heads...]
where the time goes in v1:
time: 434 us
  waiting for transfers between devices  279 us (64%)
  blocking collectives  105 us (24%)
  between operations  14.7 us (3%)
  local copies, waits for them, and re-layouts  12.7 us (3%)
  matrix products  9.26 us (2%)
  starting transfers between devices  6.93 us (2%)
  other arithmetic  5.83 us (1%)
    unnamed x5, waiting for transfers between devices  247 us
    psum x1, blocking collectives, local(): sum_squares = lax.psum(jnp.sum(stream * stream, 1), ('heads', 'side'))  46 us
    all_to_all x1, blocking collectives, local(): lax.all_to_all(jnp.stack([arrived] * lax.axis_size('heads')), 'heads', 0, 0)  44.8 us
    psum x1, waiting for transfers between devices, local(): lax.psum(up_part.astype(jnp.bfloat16), 'side').astype(jnp.float32)  25.4 us
    all_to_all x1, blocking collectives, local(): lax.all_to_all(holder.at[target].set(mixed_in[source_row]).reshape(groups...  14.1 us
  transfers between devices with their start and end apart: 4, of which 4 were waited for; matrix products, arithmetic and copies ran while one was open for 2% of the time, Pallas kernels for 0%

profile of v1, /device:TPU:32, one launch (start us, length us, event | category | flops | bytes accessed | tf_op | source)
XLA Modules:
  0.0 433.7 jit_solution(15379433573482856940)
XLA Ops:
  7.2 0.8 bitcast_convert_fusion.1
  8.1 0.7 bitcast_convert_fusion
  9.6 0.7 copy.71
  10.3 2.2 fusion.5
  12.5 1.8 fusion.8
  14.3 0.1 multiply_reduce_fusion
  14.4 0.1 rsqrt.15
  14.6 1.6 convolution_bitcast_fusion
  16.3 0.1 copy.42
  16.4 0.1 eq.15
  16.5 0.1 fusion.26
  16.6 0.1 reduce_window_sum.11
  16.7 0.1 copy.41
  16.8 0.1 mul.182
  17.0 0.8 dynamic_slice.3
  17.8 0.2 select_reduce_fusion
  17.9 110.4 %reduce-scatter.7.cloned.1.call-done = f32[96,48]{1,0:T(8,128)} async-done(((f32[3072,48]{1,0:T(8,128)}), f32[96,48]{1,0:T(8,128)}) %reduce-scatter.7.cloned.1.call-update) | async-done | bytes 18448
  128.3 0.9 copy.59
  129.2 0.1 fusion.27
  129.3 46.0 %psum.21 = f32[48]{0:T(128)S(1)} all-reduce(f32[48]{0:T(128)S(1)} %get-tuple-element.5), channel_id=1, replica_groups=mesh['dp'=16,'heads'=16,'side'=2] {'heads','side'}, use_global_device_ids=true, to_apply=%region_5.6 | all-reduce | flops 48 | bytes 384 | tf_op jit(solution)/shard_map/psum | solution.py:62
  175.3 0.1 fusion.29
  175.4 1.0 scatter_custom_fusion
  176.5 0.1 reshape.301
  176.6 14.1 %all_to_all.15 = bf16[16,2,432]{2,1,0:T(2,128)(2,1)S(1)} all-to-all(bf16[16,2,432]{2,1,0:T(2,128)(2,1)S(1)} %reshape.301), channel_id=1, replica_groups=mesh['dp'=16,'heads'=16,'side'=2] {'dp'}, dimensions={0} | all-to-all | bytes 55296 | tf_op jit(solution)/shard_map/all_to_all | solution.py:85
  190.7 0.1 reshape.302
  190.8 0.1 stack.14
  190.9 44.8 %all_to_all.16 = bf16[16,16,9,96]{3,1,2,0:T(8,128)(2,1)S(1)} all-to-all(bf16[16,16,9,96]{3,1,2,0:T(8,128)(2,1)S(1)} %stack.14), channel_id=1, replica_groups=mesh['dp'=16,'heads'=16,'side'=2] {'heads'}, dimensions={0} | all-to-all | bytes 884736 | tf_op jit(solution)/shard_map/all_to_all | solution.py:93
  235.7 0.2 copy.44
  235.9 0.6 reshape_reshape.3
  236.5 1.0 convolution_convert_fusion.1
  237.5 1.0 convolution_convert_fusion.2
  238.7 2.4 reshape_squeeze.11
  241.0 0.7 copy.45
  241.7 25.4 %all-reduce.7.cloned.1.call-done = (bf16[144,288]{1,0:T(8,128)(2,1)}, bf16[144,288]{1,0:T(8,128)(2,1)}) async-done(((bf16[144,288]{1,0:T(8,128)(2,1)}, bf16[144,288]{1,0:T(8,128)(2,1)}), (bf16[144,288]{1,0:T(8,128)(2,1)}, bf16[144,288]{1,0:T(8,128)(2,1)})) %all-reduce.7.cloned.1.call-update) | async-done | bytes 165904 | tf_op jit(solution)/shard_map/psum | solution.py:100
  267.1 1.0 fusion.23
  268.2 0.1 dot_general.29
  268.2 1.6 convolution_convert_fusion
  269.8 1.3 dynamic-slice
  271.2 1.7 fusion.4
  272.9 136.1 %all-reduce.5.cloned.1.call-done = bf16[16,9,16,96]{3,0,2,1:T(8,128)(2,1)} async-done(((bf16[16,9,16,96]{3,0,2,1:T(8,128)(2,1)}), bf16[16,9,16,96]{3,0,2,1:T(8,128)(2,1)}) %all-reduce.5.cloned.1.call-update) | async-done | bytes 442384
  409.0 1.4 constant_dynamic-slice_fusion
  410.5 0.7 reshape.303
  411.2 6.8 %all-to-all-start.2 = ((bf16[16,2,432]{2,1,0:T(2,128)(2,1)}), bf16[16,2,432]{2,1,0:T(2,128)(2,1)S(1)}, u32[]{:S(2)}, u32[]{:S(2)}) async-start(bf16[16,2,432]{2,1,0:T(2,128)(2,1)} %reshape.303), calls=%async_computation.2 | async-start | bytes 65536 | tf_op jit(solution)/shard_map/all_to_all | solution.py:109
  418.0 0.1 copy.57
  418.1 7.5 %all-to-all-done.2 = bf16[16,2,432]{2,1,0:T(2,128)(2,1)S(1)} async-done(((bf16[16,2,432]{2,1,0:T(2,128)(2,1)}), bf16[16,2,432]{2,1,0:T(2,128)(2,1)S(1)}, u32[]{:S(2)}, u32[]{:S(2)}) %all-to-all-start.2) | async-done | bytes 27680 | tf_op jit(solution)/shard_map/all_to_all | solution.py:109
  425.6 0.1 reshape.304
  425.8 0.7 gather_fusion
  426.5 0.7 fusion.25
  (40 shorter events, 0.4 us)
Async XLA Ops:
  7.2 229.3 %copy-start = (bf16[1,16,96,288]{3,2,1,0:T(8,128)(2,1)S(1)}, bf16[1,16,96,288]{3,2,1,0:T(8,128)(2,1)}, u32[]{:S(2)}) copy-start(bf16[1,16,96,288]{3,2,1,0:T(8,128)(2,1)} %param.26) | copy-start | bytes 2654212
  7.2 5.3 %copy-start.2 = (bf16[24,1,128,128]{3,2,1,0:T(8,128)(2,1)S(1)}, bf16[24,1,128,128]{3,2,1,0:T(8,128)(2,1)}, u32[]{:S(2)}) copy-start(bf16[24,1,128,128]{3,2,1,0:T(8,128)(2,1)} %param.17) | copy-start | bytes 2359300
  7.2 121.1 %reduce-scatter.7.cloned.1.call-start = ((), (), s32[]{:S(2)}) async-start(), calls=%async_computation.4 | async-start | bytes 1622016
  12.5 2.0 copy-start.4
  12.5 2.1 copy-start.9
  14.5 1.7 copy-start.7
  16.2 113.0 %copy-start.6 = (bf16[24,2,96]{2,1,0:T(2,128)(2,1)S(1)}, bf16[24,2,96]{2,1,0:T(2,128)(2,1)}, u32[]{:S(2)}) copy-start(bf16[24,2,96]{2,1,0:T(2,128)(2,1)} %param.21) | copy-start | bytes 27652
  16.2 250.9 %all-reduce.7.cloned.1.call-start = ((), (), s32[]{:S(2)}) async-start(), calls=%async_computation.6 | async-start | bytes 442368 | tf_op jit(solution)/shard_map/psum | solution.py:100
  129.3 106.5 %copy-start.5 = (bf16[48,96]{1,0:T(8,128)(2,1)}, bf16[48,96]{1,0:T(8,128)(2,1)S(1)}, u32[]{:S(2)}) copy-start(bf16[48,96]{1,0:T(8,128)(2,1)S(1)} %get-tuple-element.6) | copy-start | bytes 27652
  235.9 1.7 copy-start.1
  238.6 170.4 %all-reduce.5.cloned.1.call-start = ((), (), s32[]{:S(2)}) async-start(), calls=%async_computation.5 | async-start | bytes 1179648
  241.7 29.4 %copy-start.3 = (bf16[24,1,128,128]{3,2,1,0:T(8,128)(2,1)S(1)}, bf16[24,1,128,128]{3,2,1,0:T(8,128)(2,1)}, u32[]{:S(2)}) copy-start(bf16[24,1,128,128]{3,2,1,0:T(8,128)(2,1)} %param.17) | copy-start | bytes 2359300
  269.8 148.2 %copy-start.8 = (f32[24,2,2]{0,2,1:T(2,128)S(1)}, f32[24,2,2]{0,2,1:T(2,128)}, u32[]{:S(2)}) copy-start(f32[24,2,2]{0,2,1:T(2,128)} %param.24) | copy-start | bytes 1156
  411.2 14.4 %all-to-all-start.2 = ((bf16[16,2,432]{2,1,0:T(2,128)(2,1)}), bf16[16,2,432]{2,1,0:T(2,128)(2,1)S(1)}, u32[]{:S(2)}, u32[]{:S(2)}) async-start(bf16[16,2,432]{2,1,0:T(2,128)(2,1)} %reshape.303), calls=%async_computation.2 | async-start | bytes 65536 | tf_op jit(solution)/shard_map/all_to_all | solution.py:109
Sparse Core Ops, SparseCore 0:
  16.3 111.9 reduce-scatter.6
  238.7 28.3 all-reduce.6
  269.9 139.0 all-reduce.4
